TPU v7x, 128 devices: a whole 4x4x4 slice. The times are simulated.
128 devices in a mesh: wide: 32 (over z_hi, y, x), narrow: 4 (over z_lo, core).
Axes of the slice: x: 4, y: 4, z: 4 (z_hi: 2, z_lo: 2; z = z_hi * 2 + z_lo), core: 2. Of those that a mesh axis runs over, the one named last changes fastest.
Arguments:
- density: float32 [256, 256, 256], P('wide', 'narrow'), may hold values from -48 to 48
Outputs:
- recon_real: float32 [256, 256, 256], P('narrow', 'wide')
- recon_imag: float32 [256, 256, 256], P('narrow', 'wide')
All inputs are finite; a program needn't handle non-finite values.
Results may differ from a plain program's by a relative error of at most 0.0003.
Values sent between devices are 32-bit elements; how exact they have to be, the bound alone decides.
A program may use at most 128 MiB of HBM per device.

v0:
```python
from functools import partial
import math

import jax
import jax.numpy as jnp
from jax import lax
from jax.sharding import PartitionSpec as P


def tables(length):
    indices = jnp.arange(length, dtype=jnp.int32)
    products = indices[:, None] * indices[None, :] % length
    angles = products.astype(jnp.float32) * (2.0 * math.pi / length)
    return (jnp.cos(angles), jnp.sin(angles))


def transform(parts_in, position, inverse, pattern_last=False):
    real_part, imag_part = parts_in
    length = real_part.shape[position]
    cosine, sine = tables(length)
    if position == 1:
        pattern = "fabc,ad->fcbd" if pattern_last else "fabc,ad->fdbc"
    elif position == 2:
        pattern = "fabc,bd->fadc"
    else:
        pattern = "fabc,cd->fabd"
    contract = partial(
        jnp.einsum, pattern, precision=lax.Precision.HIGHEST, preferred_element_type=jnp.float32
    )
    real_cos = contract(real_part, cosine)
    real_sin = contract(real_part, sine)
    imag_cos = contract(imag_part, cosine)
    imag_sin = contract(imag_part, sine)
    if inverse:
        scale = 1.0 / length
        return ((real_cos - imag_sin) * scale, (imag_cos + real_sin) * scale)
    return (real_cos + imag_sin, imag_cos - real_sin)


def pass_second(parts_in):
    return transform(parts_in, 2, False)


def pass_first(parts_in):
    return transform(parts_in, 1, False)


def pass_first_last(parts_in):
    return transform(parts_in, 1, False, True)


def back_second(parts_in):
    return transform(parts_in, 2, True)


def back_third(parts_in):
    return transform(parts_in, 3, True)


def forward(real_part, imag_part, first_last):
    section = transform((real_part, imag_part), 3, False)
    section = pass_second(
        (
            lax.all_to_all(section[0], "narrow", split_axis=3, concat_axis=2, tiled=True),
            lax.all_to_all(section[1], "narrow", split_axis=3, concat_axis=2, tiled=True),
        )
    )
    final_pass = pass_first_last if first_last else pass_first
    section = final_pass(
        (
            lax.all_to_all(section[0], "wide", split_axis=2, concat_axis=1, tiled=True),
            lax.all_to_all(section[1], "wide", split_axis=2, concat_axis=1, tiled=True),
        )
    )
    return section


def inverse(real_part, imag_part):
    section = transform((real_part, imag_part), 1, True)
    section = back_second(
        (
            lax.all_to_all(section[0], "wide", split_axis=1, concat_axis=2, tiled=True),
            lax.all_to_all(section[1], "wide", split_axis=1, concat_axis=2, tiled=True),
        )
    )
    section = back_third(
        (
            lax.all_to_all(section[0], "narrow", split_axis=2, concat_axis=3, tiled=True),
            lax.all_to_all(section[1], "narrow", split_axis=2, concat_axis=3, tiled=True),
        )
    )
    return section


def wavenumbers(length, offset, count):
    indices = offset + jnp.arange(count, dtype=jnp.int32)
    signed = jnp.where(indices < length // 2, indices, indices - length)
    wave = signed.astype(jnp.float32) * (2.0 * math.pi / length)
    return (wave, indices != length // 2, indices == 0)


def per_device(density):
    length = density.shape[2]
    zeros_in = jnp.zeros((1,) + density.shape, jnp.float32)
    spec_real, spec_imag = forward(density[None], zeros_in, False)
    spec_real = spec_real[0]
    spec_imag = spec_imag[0]
    rows_y = spec_real.shape[1]
    rows_z = spec_real.shape[2]
    wave_x, usable_x, anchor_x = wavenumbers(length, 0, length)
    wave_y, usable_y, anchor_y = wavenumbers(length, lax.axis_index("wide") * rows_y, rows_y)
    wave_z, usable_z, anchor_z = wavenumbers(length, lax.axis_index("narrow") * rows_z, rows_z)
    wave_x = wave_x[:, None, None]
    wave_y = wave_y[None, :, None]
    wave_z = wave_z[None, None, :]
    squared = wave_x * wave_x + wave_y * wave_y + wave_z * wave_z
    keep = (
        usable_x[:, None, None] & usable_y[None, :, None] & usable_z[None, None, :] & (squared > 0)
    )
    squared_safe = jnp.where(squared > 0, squared, jnp.ones_like(squared))
    smooth_kernel = jnp.where(keep, jnp.exp(-0.5 * squared) / squared_safe, jnp.zeros_like(squared))
    waves = [wave_x, wave_y, wave_z]
    pairs = [(0, 0), (1, 1), (2, 2), (0, 1), (0, 2), (1, 2)]
    kernels = [smooth_kernel * waves[first] * waves[second] for first, second in pairs]
    stacked_real = jnp.stack([kernel * spec_real for kernel in kernels])
    stacked_imag = jnp.stack([kernel * spec_imag for kernel in kernels])
    tidal_real, tidal_imag = inverse(stacked_real, stacked_imag)
    tidal = [tidal_real[number] for number in range(6)]
    shear = tidal[0] * tidal[0] + tidal[1] * tidal[1] + tidal[2] * tidal[2]
    shear = shear + 2.0 * (tidal[3] * tidal[3] + tidal[4] * tidal[4] + tidal[5] * tidal[5])
    recon_real, recon_imag = forward(shear[None], zeros_in, True)
    norm_scale = 1.0 / float(length) ** 1.5
    anchor = anchor_z[:, None, None] & anchor_y[None, :, None] & anchor_x[None, None, :]
    recon_real = jnp.where(anchor, 0.0, recon_real[0] * norm_scale).astype(jnp.float32)
    recon_imag = jnp.where(anchor, 0.0, recon_imag[0] * norm_scale).astype(jnp.float32)
    return (recon_real, recon_imag)


def solution(mesh):
    in_specs = (P("wide", "narrow", None),)
    out_specs = (P("narrow", "wide", None), P("narrow", "wide", None))
    return jax.shard_map(
        per_device, mesh=mesh, in_specs=in_specs, out_specs=out_specs, check_vma=False
    )
```

profile of v0, /device:TPU:0, one launch (start us, length us, event | category | flops | bytes accessed | tf_op | source)
XLA Modules:
  0.0 476.6 jit_solution(14756458941035715394)
XLA Ops:
  5.7 3.5 all-to-all-start
  15.2 2.7 all-to-all-done
  17.9 4.6 all-to-all-start.1
  23.1 2.1 reduce
  27.0 2.4 fusion.103
  29.4 2.4 fusion.81
  31.7 3.0 reduce.1
  41.4 10.7 %all-to-all-start.3 = ((f32[32,1,4096]{2,1,0:T(1,128)}), f32[32,1,4096]{2,1,0:T(1,128)S(1)}, u32[]{:S(2)}, u32[]{:S(2)}) async-start(f32[32,1,4096]{2,1,0:T(1,128)} %reshape.353), calls=%async_computation.3 | async-start | bytes 1048576 | tf_op jit(solution)/shard_map/all_to_all | solution.py:72
  52.1 2.6 fusion.105
  56.7 9.0 %all-to-all-done.3 = f32[32,1,4096]{2,1,0:T(1,128)S(1)} async-done(((f32[32,1,4096]{2,1,0:T(1,128)}), f32[32,1,4096]{2,1,0:T(1,128)S(1)}, u32[]{:S(2)}, u32[]{:S(2)}) %all-to-all-start.3) | async-done | bytes 524320 | tf_op jit(solution)/shard_map/all_to_all | solution.py:72
  65.7 4.3 all-to-all-start.2
  70.0 1.8 reduce.3
  74.5 2.4 fusion.101
  76.9 5.0 %all-to-all-done.2 = f32[32,1,4096]{2,1,0:T(1,128)S(1)} async-done(((f32[32,1,4096]{2,1,0:T(1,128)}), f32[32,1,4096]{2,1,0:T(1,128)S(1)}, u32[]{:S(2)}, u32[]{:S(2)}) %all-to-all-start.2) | async-done | bytes 524320 | tf_op jit(solution)/shard_map/all_to_all | solution.py:71
  91.1 3.6 fusion.68
  94.7 3.6 fusion.95
  98.4 2.5 multiply_bitcast_fusion.2
  100.9 7.0 %copy.67 = f32[6,256,8,64]{3,2,0,1:T(8,128)} copy(f32[6,256,8,64]{1,3,2,0:T(8,128)} %multiply_bitcast_fusion.2) | data formatting | bytes 6291456 | tf_op jit(solution)/shard_map/mul | solution.py:36
  107.8 7.4 %reshape.357 = f32[32,1,24576]{2,1,0:T(1,128)} reshape(f32[256,6,8,64]{3,2,1,0:T(8,128)} %bitcast.304) | data formatting | bytes 6291456
  115.2 5.1 %all-to-all-start.5 = ((f32[32,1,24576]{2,1,0:T(1,128)}), f32[32,1,24576]{2,1,0:T(1,128)}, u32[]{:S(2)}, u32[]{:S(2)}) async-start(f32[32,1,24576]{2,1,0:T(1,128)} %reshape.357), calls=%async_computation.5 | async-start | bytes 6291456 | tf_op jit(solution)/shard_map/all_to_all | solution.py:83
  120.4 5.7 %fusion.97 = f32[256,3072]{0,1:S(1)} fusion(f32[256,3072]{0,1:T(8,128)} %bitcast.315), kind=kOutput, calls=%fused_computation.118 | convolution fusion | flops 2416836608 | bytes 6291456
  126.1 3.6 fusion.73
  129.7 2.5 multiply_bitcast_fusion.3
  132.1 7.0 %copy.63 = f32[6,256,8,64]{3,2,0,1:T(8,128)} copy(f32[6,256,8,64]{1,3,2,0:T(8,128)} %multiply_bitcast_fusion.3) | data formatting | bytes 6291456 | tf_op jit(solution)/shard_map/mul | solution.py:36
  139.1 7.4 %reshape.359 = f32[32,1,24576]{2,1,0:T(1,128)} reshape(f32[256,6,8,64]{3,2,1,0:T(8,128)} %bitcast.305) | data formatting | bytes 6291456
  146.5 13.2 %all-to-all-done.5 = f32[32,1,24576]{2,1,0:T(1,128)} async-done(((f32[32,1,24576]{2,1,0:T(1,128)}), f32[32,1,24576]{2,1,0:T(1,128)}, u32[]{:S(2)}, u32[]{:S(2)}) %all-to-all-start.5) | async-done | bytes 3145760 | tf_op jit(solution)/shard_map/all_to_all | solution.py:83
  159.7 6.4 %all-to-all-start.4 = ((f32[32,1,24576]{2,1,0:T(1,128)}), f32[32,1,24576]{2,1,0:T(1,128)}, u32[]{:S(2)}, u32[]{:S(2)}) async-start(f32[32,1,24576]{2,1,0:T(1,128)} %reshape.359), calls=%async_computation.4 | async-start | bytes 6291456 | tf_op jit(solution)/shard_map/all_to_all | solution.py:82
  166.1 11.8 %reduce.4 = f32[32,24576]{1,0:T(8,128)} reduce(f32[32,1,24576]{2,1,0:T(1,128)} %all-to-all-done.5, f32[]{:T(128)} %broadcast.580), dimensions={1}, to_apply=%all_to_all.156.reduce_sub_computation | reduce | bytes 6291460 | tf_op jit(solution)/shard_map/all_to_all | solution.py:83
  177.9 6.6 %reshape.358 = f32[256,6,8,64]{3,2,1,0:T(8,128)} reshape(f32[32,24576]{1,0:T(8,128)} %reduce.4) | data formatting | bytes 6291456
  184.5 15.2 %fusion.2 = f32[256,6,8,64]{0,3,2,1:T(8,128)} fusion(f32[6,8,32,8,64]{4,3,0,1,2:T(8,128)} %bitcast.298), kind=kOutput, calls=%fused_computation.2 | convolution fusion | flops 2416836608 | bytes 6291456 | tf_op jit(solution)/shard_map/fabc,bd->fadc/dot_general | solution.py:33
  199.7 7.0 %all-to-all-done.4 = f32[32,1,24576]{2,1,0:T(1,128)} async-done(((f32[32,1,24576]{2,1,0:T(1,128)}), f32[32,1,24576]{2,1,0:T(1,128)}, u32[]{:S(2)}, u32[]{:S(2)}) %all-to-all-start.4) | async-done | bytes 3145760 | tf_op jit(solution)/shard_map/all_to_all | solution.py:82
  206.7 12.0 %reduce.5 = f32[32,24576]{1,0:T(8,128)} reduce(f32[32,1,24576]{2,1,0:T(1,128)} %all-to-all-done.4, f32[]{:T(128)} %broadcast.580), dimensions={1}, to_apply=%all_to_all.152.reduce_sub_computation | reduce | bytes 6291460 | tf_op jit(solution)/shard_map/all_to_all | solution.py:82
  218.7 6.1 %reshape.360 = f32[256,6,8,64]{3,2,1,0:T(8,128)} reshape(f32[32,24576]{1,0:T(8,128)} %reduce.5) | data formatting | bytes 6291456
  224.8 16.1 %multiply_bitcast_fusion.1 = f32[6,8,256,64]{2,3,1,0:T(8,128)} fusion(f32[256,6,8,64]{0,3,2,1:T(8,128)} %fusion.2, f32[6,8,32,8,64]{4,3,0,1,2:T(8,128)} %bitcast.300), kind=kOutput, calls=%fused_computation.16 | convolution fusion | flops 2418409472 | bytes 9437184 | tf_op jit(solution)/shard_map/fabc,bd->fadc/dot_general | solution.py:30
  240.9 6.9 %copy.71 = f32[6,8,256,64]{3,1,0,2:T(8,128)} copy(f32[6,8,256,64]{2,3,1,0:T(8,128)} %multiply_bitcast_fusion.1) | data formatting | bytes 6291456 | tf_op jit(solution)/shard_map/mul | solution.py:36
  247.8 7.1 %reshape.361 = f32[4,1,196608]{2,1,0:T(1,128)} reshape(f32[256,6,8,64]{3,2,1,0:T(8,128)} %bitcast.306) | data formatting | bytes 6291456
  254.9 5.2 %all-to-all-start.6 = ((f32[4,1,196608]{2,1,0:T(1,128)}), f32[4,1,196608]{2,1,0:T(1,128)}, u32[]{:S(2)}, u32[]{:S(2)}) async-start(f32[4,1,196608]{2,1,0:T(1,128)} %reshape.361), calls=%async_computation.6 | async-start | bytes 6291456 | tf_op jit(solution)/shard_map/all_to_all | solution.py:88
  260.1 13.9 %fusion = f32[256,6,8,64]{0,3,2,1:T(8,128)S(1)} fusion(f32[6,8,32,8,64]{4,3,0,1,2:T(8,128)} %bitcast.299), kind=kOutput, calls=%fused_computation | convolution fusion | flops 2416836608 | bytes 6291456 | tf_op jit(solution)/shard_map/fabc,bd->fadc/dot_general | solution.py:32
  274.1 12.7 %multiply_bitcast_fusion = f32[6,8,256,64]{2,3,1,0:T(8,128)} fusion(f32[256,6,8,64]{0,3,2,1:T(8,128)S(1)} %fusion, f32[6,8,32,8,64]{4,3,0,1,2:T(8,128)S(1)} %bitcast.303), kind=kOutput, calls=%fused_computation.15 | convolution fusion | flops 2418409472 | bytes 9437184 | tf_op jit(solution)/shard_map/fabc,bd->fadc/dot_general | solution.py:31
  286.8 7.0 %copy.75 = f32[6,8,256,64]{3,1,0,2:T(8,128)} copy(f32[6,8,256,64]{2,3,1,0:T(8,128)} %multiply_bitcast_fusion) | data formatting | bytes 6291456 | tf_op jit(solution)/shard_map/mul | solution.py:36
  293.8 7.1 %reshape.363 = f32[4,1,196608]{2,1,0:T(1,128)} reshape(f32[256,6,8,64]{3,2,1,0:T(8,128)} %bitcast.307) | data formatting | bytes 6291456
  300.9 4.9 %all-to-all-start.7 = ((f32[4,1,196608]{2,1,0:T(1,128)}), f32[4,1,196608]{2,1,0:T(1,128)}, u32[]{:S(2)}, u32[]{:S(2)}) async-start(f32[4,1,196608]{2,1,0:T(1,128)} %reshape.363), calls=%async_computation.7 | async-start | bytes 6291456 | tf_op jit(solution)/shard_map/all_to_all | solution.py:89
  305.8 11.6 %reduce.6 = f32[4,196608]{1,0:T(4,128)} reduce(f32[4,1,196608]{2,1,0:T(1,128)} %all-to-all-done.6, f32[]{:T(128)} %broadcast.580), dimensions={1}, to_apply=%all_to_all.160.reduce_sub_computation | reduce | bytes 6291460 | tf_op jit(solution)/shard_map/all_to_all | solution.py:88
  317.4 7.4 %reshape.362 = f32[256,6,8,64]{3,2,1,0:T(8,128)} reshape(f32[4,196608]{1,0:T(4,128)} %reduce.6) | data formatting | bytes 6291456
  324.8 9.5 %copy.132 = f32[6,8,4,64,64]{4,2,3,1,0:T(4,128)} copy(f32[6,8,4,64,64]{4,1,0,3,2:T(8,128)} %bitcast.308) | data formatting | bytes 6291456 | tf_op jit(solution)/shard_map/all_to_all | solution.py:88
  334.3 7.3 %all_to_all.163 = f32[6,8,64,256]{3,2,1,0:T(8,128)} reshape(f32[6,8,64,4,64]{4,3,2,1,0:T(4,128)} %bitcast.309) | data formatting | bytes 6291456 | tf_op jit(solution)/shard_map/all_to_all | solution.py:88
  341.6 7.2 %fusion.40 = f32[6,8,64,256]{3,2,1,0:T(8,128)} fusion(f32[6,8,64,256]{3,2,1,0:T(8,128)} %all_to_all.163), kind=kOutput, calls=%fused_computation.86 | convolution fusion | flops 2416836608 | bytes 6291456 | tf_op jit(solution)/shard_map/fabc,cd->fabd/dot_general | solution.py:30
  348.8 11.6 %reduce.7 = f32[4,196608]{1,0:T(4,128)} reduce(f32[4,1,196608]{2,1,0:T(1,128)} %all-to-all-done.7, f32[]{:T(128)} %broadcast.580), dimensions={1}, to_apply=%all_to_all.164.reduce_sub_computation | reduce | bytes 6291460 | tf_op jit(solution)/shard_map/all_to_all | solution.py:89
  360.4 7.4 %reshape.364 = f32[256,6,8,64]{3,2,1,0:T(8,128)} reshape(f32[4,196608]{1,0:T(4,128)} %reduce.7) | data formatting | bytes 6291456
  367.8 9.5 %copy.131 = f32[6,8,4,64,64]{4,2,3,1,0:T(4,128)} copy(f32[6,8,4,64,64]{4,1,0,3,2:T(8,128)} %bitcast.310) | data formatting | bytes 6291456 | tf_op jit(solution)/shard_map/all_to_all | solution.py:89
  377.3 7.1 %all_to_all.167 = f32[6,8,64,256]{3,2,1,0:T(8,128)} reshape(f32[6,8,64,4,64]{4,3,2,1,0:T(4,128)} %bitcast.311) | data formatting | bytes 6291456 | tf_op jit(solution)/shard_map/all_to_all | solution.py:89
  384.4 6.6 %subtract_multiply_fusion = f32[6,8,64,256]{3,2,1,0:T(8,128)S(1)} fusion(f32[6,8,64,256]{3,2,1,0:T(8,128)} %fusion.40, f32[6,8,64,256]{3,2,1,0:T(8,128)} %all_to_all.167), kind=kOutput, calls=%fused_computation.14 | convolution fusion | flops 2418409472 | bytes 9437184 | tf_op jit(solution)/shard_map/fabc,cd->fabd/dot_general | solution.py:33
  394.6 3.5 all-to-all-start.8
  401.6 5.3 %all-to-all-done.8 = f32[4,1,32768]{2,1,0:T(1,128)S(1)} async-done(((f32[4,1,32768]{2,1,0:T(1,128)}), f32[4,1,32768]{2,1,0:T(1,128)S(1)}, u32[]{:S(2)}, u32[]{:S(2)}) %all-to-all-start.8) | async-done | bytes 524320 | tf_op jit(solution)/shard_map/all_to_all | solution.py:64
  406.9 4.6 all-to-all-start.9
  411.5 2.1 reduce.9
  415.4 2.4 fusion.90
  419.9 3.0 reduce.8
  429.4 6.7 %all-to-all-start.11 = ((f32[32,1,4096]{2,1,0:T(1,128)}), f32[32,1,4096]{2,1,0:T(1,128)S(1)}, u32[]{:S(2)}, u32[]{:S(2)}) async-start(f32[32,1,4096]{2,1,0:T(1,128)} %reshape.371), calls=%async_computation.11 | async-start | bytes 1048576 | tf_op jit(solution)/shard_map/all_to_all | solution.py:72
  439.7 9.3 %all-to-all-done.11 = f32[32,1,4096]{2,1,0:T(1,128)S(1)} async-done(((f32[32,1,4096]{2,1,0:T(1,128)}), f32[32,1,4096]{2,1,0:T(1,128)S(1)}, u32[]{:S(2)}, u32[]{:S(2)}) %all-to-all-start.11) | async-done | bytes 524320 | tf_op jit(solution)/shard_map/all_to_all | solution.py:72
  448.9 4.6 all-to-all-start.10
  459.7 5.2 %all-to-all-done.10 = f32[32,1,4096]{2,1,0:T(1,128)S(1)} async-done(((f32[32,1,4096]{2,1,0:T(1,128)}), f32[32,1,4096]{2,1,0:T(1,128)S(1)}, u32[]{:S(2)}, u32[]{:S(2)}) %all-to-all-start.10) | async-done | bytes 524320 | tf_op jit(solution)/shard_map/all_to_all | solution.py:71
  468.6 2.7 fusion.107
  471.3 2.6 fusion.64
  (121 shorter events, 67.0 us)
Async XLA Ops:
  0.6 1.6 copy-start
  5.7 12.3 %all-to-all-start = ((f32[4,1,32768]{2,1,0:T(1,128)}), f32[4,1,32768]{2,1,0:T(1,128)S(1)}, u32[]{:S(2)}, u32[]{:S(2)}) async-start(f32[4,1,32768]{2,1,0:T(1,128)} %reshape.351), calls=%async_computation | async-start | bytes 1048576 | tf_op jit(solution)/shard_map/all_to_all | solution.py:64
  10.8 0.8 copy-start.5
  17.9 13.8 %all-to-all-start.1 = ((f32[4,1,32768]{2,1,0:T(1,128)}), f32[4,1,32768]{2,1,0:T(1,128)}, u32[]{:S(2)}, u32[]{:S(2)}) async-start(f32[4,1,32768]{2,1,0:T(1,128)} %reshape.349), calls=%async_computation.1 | async-start | bytes 1048576 | tf_op jit(solution)/shard_map/all_to_all | solution.py:65
  36.6 1.6 copy-start.9
  38.2 16.6 %copy-start.7 = (f32[256,512]{0,1:S(1)}, f32[256,512]{0,1}, u32[]{:S(2)}) copy-start(f32[256,512]{0,1} %fusion.81) | copy-start | bytes 1572868
  41.4 24.3 %all-to-all-start.3 = ((f32[32,1,4096]{2,1,0:T(1,128)}), f32[32,1,4096]{2,1,0:T(1,128)S(1)}, u32[]{:S(2)}, u32[]{:S(2)}) async-start(f32[32,1,4096]{2,1,0:T(1,128)} %reshape.353), calls=%async_computation.3 | async-start | bytes 1048576 | tf_op jit(solution)/shard_map/all_to_all | solution.py:72
  65.7 16.2 %all-to-all-start.2 = ((f32[32,1,4096]{2,1,0:T(1,128)}), f32[32,1,4096]{2,1,0:T(1,128)S(1)}, u32[]{:S(2)}, u32[]{:S(2)}) async-start(f32[32,1,4096]{2,1,0:T(1,128)} %reshape.355), calls=%async_computation.2 | async-start | bytes 1048576 | tf_op jit(solution)/shard_map/all_to_all | solution.py:71
  84.3 3.7 copy-start.8
  91.1 3.6 copy-start.4
  91.1 3.6 copy-start.2
  115.2 44.5 %all-to-all-start.5 = ((f32[32,1,24576]{2,1,0:T(1,128)}), f32[32,1,24576]{2,1,0:T(1,128)}, u32[]{:S(2)}, u32[]{:S(2)}) async-start(f32[32,1,24576]{2,1,0:T(1,128)} %reshape.357), calls=%async_computation.5 | async-start | bytes 6291456 | tf_op jit(solution)/shard_map/all_to_all | solution.py:83
  120.4 5.7 %copy-start.3 = (f32[6,256,8,64]{1,3,2,0:T(8,128)S(1)}, f32[6,256,8,64]{1,3,2,0:T(8,128)}, u32[]{:S(2)}) copy-start(f32[6,256,8,64]{1,3,2,0:T(8,128)} %copy-done.2) | copy-start | bytes 9437188
  159.7 47.0 %all-to-all-start.4 = ((f32[32,1,24576]{2,1,0:T(1,128)}), f32[32,1,24576]{2,1,0:T(1,128)}, u32[]{:S(2)}, u32[]{:S(2)}) async-start(f32[32,1,24576]{2,1,0:T(1,128)} %reshape.359), calls=%async_computation.4 | async-start | bytes 6291456 | tf_op jit(solution)/shard_map/all_to_all | solution.py:82
  254.9 19.2 %slice-start = ((s8[6291456]{0:T(1024)(128)(4,1)}), s8[2097152]{0:T(1024)(128)(4,1)S(1)}, s32[]{:S(2)}) async-start(s8[6291456]{0:T(1024)(128)(4,1)} %bitcast.301), calls=%async_computation.12 | async-start | bytes 4194304
  254.9 45.9 %all-to-all-start.6 = ((f32[4,1,196608]{2,1,0:T(1,128)}), f32[4,1,196608]{2,1,0:T(1,128)}, u32[]{:S(2)}, u32[]{:S(2)}) async-start(f32[4,1,196608]{2,1,0:T(1,128)} %reshape.361), calls=%async_computation.6 | async-start | bytes 6291456 | tf_op jit(solution)/shard_map/all_to_all | solution.py:88
  260.1 14.0 %slice-start.1 = ((s8[6291456]{0:T(1024)(128)(4,1)}), s8[4194304]{0:T(1024)(128)(4,1)S(1)}, s32[]{:S(2)}) async-start(s8[6291456]{0:T(1024)(128)(4,1)} %bitcast.301), calls=%async_computation.13 | async-start | bytes 8388608
  300.9 47.9 %all-to-all-start.7 = ((f32[4,1,196608]{2,1,0:T(1,128)}), f32[4,1,196608]{2,1,0:T(1,128)}, u32[]{:S(2)}, u32[]{:S(2)}) async-start(f32[4,1,196608]{2,1,0:T(1,128)} %reshape.363), calls=%async_computation.7 | async-start | bytes 6291456 | tf_op jit(solution)/shard_map/all_to_all | solution.py:89
  391.2 7.0 %copy-start.6 = (f32[8,64,256]{2,1,0:T(8,128)S(1)}, f32[8,64,256]{2,1,0:T(8,128)}, u32[]{:S(2)}) copy-start(f32[8,64,256]{2,1,0:T(8,128)} %copy-done.5) | copy-start | bytes 1572868
  394.6 12.3 %all-to-all-start.8 = ((f32[4,1,32768]{2,1,0:T(1,128)}), f32[4,1,32768]{2,1,0:T(1,128)S(1)}, u32[]{:S(2)}, u32[]{:S(2)}) async-start(f32[4,1,32768]{2,1,0:T(1,128)} %reshape.365), calls=%async_computation.8 | async-start | bytes 1048576 | tf_op jit(solution)/shard_map/all_to_all | solution.py:64
  406.9 13.0 %all-to-all-start.9 = ((f32[4,1,32768]{2,1,0:T(1,128)}), f32[4,1,32768]{2,1,0:T(1,128)}, u32[]{:S(2)}, u32[]{:S(2)}) async-start(f32[4,1,32768]{2,1,0:T(1,128)} %reshape.367), calls=%async_computation.9 | async-start | bytes 1048576 | tf_op jit(solution)/shard_map/all_to_all | solution.py:65
  424.8 1.6 copy-start.10
  426.4 9.8 %copy-start.11 = (f32[8,256,64]{1,2,0:T(8,128)S(1)}, f32[8,256,64]{1,2,0:T(8,128)}, u32[]{:S(2)}) copy-start(f32[8,256,64]{1,2,0:T(8,128)} %copy-done.10) | copy-start | bytes 1572868
  429.4 19.5 %all-to-all-start.11 = ((f32[32,1,4096]{2,1,0:T(1,128)}), f32[32,1,4096]{2,1,0:T(1,128)S(1)}, u32[]{:S(2)}, u32[]{:S(2)}) async-start(f32[32,1,4096]{2,1,0:T(1,128)} %reshape.371), calls=%async_computation.11 | async-start | bytes 1048576 | tf_op jit(solution)/shard_map/all_to_all | solution.py:72
  448.9 15.9 %all-to-all-start.10 = ((f32[32,1,4096]{2,1,0:T(1,128)}), f32[32,1,4096]{2,1,0:T(1,128)S(1)}, u32[]{:S(2)}, u32[]{:S(2)}) async-start(f32[32,1,4096]{2,1,0:T(1,128)} %reshape.369), calls=%async_computation.10 | async-start | bytes 1048576 | tf_op jit(solution)/shard_map/all_to_all | solution.py:71
  468.6 7.8 %copy-start.1 = (f32[8,64,256]{2,1,0:T(8,128)S(1)}, f32[8,64,256]{2,1,0:T(8,128)}, u32[]{:S(2)}) copy-start(f32[8,64,256]{2,1,0:T(8,128)} %param.1) | copy-start | bytes 1572868
where the time goes:
time: 486 us; the launch traced here: 477 us
  local copies, waits for them, and re-layouts  149 us (31%)
  matrix products  129 us (27%)
  other arithmetic  75.6 us (16%)
  starting transfers between devices  64 us (13%)
  waiting for transfers between devices  57.2 us (12%)
    unnamed x54, local copies, waits for them, and re-layouts  75 us
    unnamed x20, matrix products  48.1 us
    mul x4, local copies, waits for them, and re-layouts, transform(): return ((real_cos - imag_sin) * scale, (imag_cos + real_sin) * scale)  27.8 us
    dot_general x4, matrix products, transform(): real_cos = contract(real_part, cosine)  26.4 us
    dot_general x3, matrix products, transform(): imag_sin = contract(imag_part, sine)  23.4 us
    all_to_all x2, waiting for transfers between devices, forward(): lax.all_to_all(section[1], 'wide', split_axis=2, concat_axis=1, tiled=True)  18.3 us
    all_to_all x2, starting transfers between devices, forward(): lax.all_to_all(section[1], 'wide', split_axis=2, concat_axis=1, tiled=True)  17.5 us
    all_to_all x2, local copies, waits for them, and re-layouts, inverse(): lax.all_to_all(section[0], 'narrow', split_axis=2, concat_axis=3, tiled=T...  16.8 us
  transfers between devices with their start and end apart: 12, of which 9 were waited for; matrix products, arithmetic and copies ran while one was open for 38% of the time, Pallas kernels for 0%

commit v1 on v0

v1 whole, which is shorter than its diff:
```python
import math

import jax
import jax.numpy as jnp
import ml_dtypes
import numpy as np
from jax import lax
from jax.experimental import pallas as pl
from jax.experimental.pallas import tpu as pltpu
from jax.sharding import PartitionSpec as P

MESH = pl.DeviceIdType.MESH
BF16 = jnp.bfloat16
F32 = jnp.float32
N = 256
H = 128
STEP = 2.0 * math.pi / N
NUM = 128


def split_np(table):
    table = np.asarray(table, np.float32)
    high = table.astype(ml_dtypes.bfloat16)
    low = (table - high.astype(np.float32)).astype(ml_dtypes.bfloat16)
    return high, low


def angle(rows, cols):
    return (np.asarray(rows)[:, None] * np.asarray(cols)[None, :] % N) * STEP


def tables():
    half = np.arange(H)
    full = np.arange(N)
    slab = np.concatenate([half, [H], N - half[1:]])
    wave = half * STEP
    weight = np.where(half == 0, 1.0, 2.0) / N
    cos_sin = np.concatenate([np.cos(angle(half, full)), np.sin(angle(half, full))])

    def back(points, power):
        cosine = np.cos(angle(points, half)) * (weight * wave**power)
        sine = np.sin(angle(points, half)) * (weight * wave**power)
        if power == 1:
            return np.concatenate([sine, -cosine], axis=1)
        return np.concatenate([cosine, sine], axis=1)

    back_slab = [back(slab, power) for power in range(3)]
    back_full = [back(full, power) for power in range(3)]
    pieces = []
    for part in range(4):
        cols = 64 * part + np.arange(64)
        pieces += [np.cos(angle(full, cols)), -np.sin(angle(full, cols))]
    last_z = np.concatenate(pieces, axis=1)
    last_y = np.concatenate([np.cos(angle(full, full)), np.sin(angle(full, full))])
    even = np.cos(angle(half, full))
    odd = np.sin(angle(half, full))
    odd[0] = np.where(full % 2 == 0, 1.0, -1.0)
    last_x = np.concatenate([even, odd]) / float(N) ** 1.5
    out = []
    for table in [cos_sin] + back_slab + back_full + [last_z, last_y, last_x]:
        out += list(split_np(table))
    return out


def split(value):
    high = value.astype(BF16)
    low = (value - high.astype(F32)).astype(BF16)
    return high, low


def product(left, right, dims):
    def one(a, b):
        return lax.dot_general(a, b, (dims, ((), ())), preferred_element_type=F32)

    return one(left[0], right[0]) + (one(left[0], right[1]) + one(left[1], right[0]))


ROW_COL = ((1,), (0,))
ROW_ROW = ((1,), (1,))
COL_COL = ((0,), (0,))
PAIRS = ((0, 0, 1.0), (0, 1, 2.0), (0, 2, 1.0), (1, 0, 2.0), (1, 1, 2.0), (2, 0, 1.0))


def device(place):
    return {"wide": place // 4, "narrow": place % 4}


def body(density, *refs):
    consts, refs = refs[:20], refs[20:]
    real_out, imag_out, refs = refs[0], refs[1], refs[2:]
    (tabs, refs) = refs[:20], refs[20:]
    send1, recv1 = refs[0], refs[1]
    send2, recv2 = refs[2:5], refs[5:8]
    send3, recv3 = refs[8:10], refs[10:12]
    final = refs[12:16]
    shear_ref, load_sem, store_sem, sent, got = refs[16:]
    wide = lax.axis_index("wide")
    narrow = lax.axis_index("narrow")
    me = wide * 4 + narrow

    barrier = pltpu.get_barrier_semaphore()

    def greet(step, carry):
        pl.semaphore_signal(
            barrier, inc=1, device_id=device((me + step) % NUM), device_id_type=MESH
        )
        return carry

    lax.fori_loop(1, NUM, greet, 0)
    loads = [
        pltpu.make_async_copy(consts[i], tabs[i], load_sem.at[i]) for i in range(20)
    ]
    for load in loads:
        load.start()

    def table(number):
        return tabs[2 * number][...], tabs[2 * number + 1][...]

    def ready(number):
        loads[2 * number].wait()
        loads[2 * number + 1].wait()

    def exchange(source, target, mine_from, mine_to, phase):
        pltpu.make_async_copy(mine_from, mine_to, got.at[phase]).start()

        def start(step, carry):
            place = (me + step * 37) % NUM
            pltpu.make_async_remote_copy(
                src_ref=source(place),
                dst_ref=target,
                send_sem=sent.at[phase],
                recv_sem=got.at[phase],
                device_id=device(place),
                device_id_type=MESH,
            ).start()
            return carry

        lax.fori_loop(1, NUM, start, 0)

    def rows(ref, place):
        return ref.at[pl.ds(pl.multiple_of(place * 8, 8), 8)]

    ready(0)
    block = split(density[...].reshape(512, N))
    lines = product(table(0), block, ROW_ROW)
    for x in range(8):
        send1[pl.ds(x, H, stride=8), :] = jnp.concatenate(
            [lines[:H, 64 * x : 64 * x + 64], lines[H:, 64 * x : 64 * x + 64]], axis=1
        )
    pl.semaphore_wait(barrier, NUM - 1)
    landing = recv1.at[wide, pl.ds(pl.multiple_of(narrow * 8, 8), 8)]
    exchange(lambda place: rows(send1, place), landing, rows(send1, me), landing, 0)

    for number in range(1, 10):
        ready(number)
    wave_a = lax.broadcasted_iota(jnp.int32, (H, H), 0).astype(F32) * STEP
    wave_b = lax.broadcasted_iota(jnp.int32, (H, H), 1).astype(F32) * STEP
    wave_c = me.astype(F32) * STEP
    squared = wave_a * wave_a + wave_b * wave_b + wave_c * wave_c
    smooth = jnp.where(
        squared > 0, jnp.exp(-0.5 * squared) / jnp.where(squared > 0, squared, 1.0), 0.0
    )
    smooth = jnp.concatenate([smooth, smooth], axis=0)
    smooth = jnp.concatenate([smooth] * 4, axis=1)

    pltpu.make_async_copy(recv1, recv1, got.at[0]).wait()
    quarter = [recv1[:, 8 * n : 8 * n + 8, :].reshape(N, H) for n in range(4)]
    plane = jnp.concatenate(
        [q[:, :64] for q in quarter] + [q[:, 64:] for q in quarter], axis=1
    )
    along_x = product(table(0), split(plane), ROW_COL)
    along_x = jnp.concatenate([along_x[:, :N], along_x[:, N:]], axis=0)
    along_y = product(split(along_x), table(0), ROW_ROW)
    spectrum = jnp.concatenate([along_y[:N], along_y[N:]], axis=1)
    filtered = split(spectrum * smooth)
    for power in range(3):
        field = product(table(1 + power), filtered, ROW_COL)
        for x1 in range(2):
            for kind in range(4):
                send2[power][pl.ds(4 * x1 + kind, H, stride=8), :] = field[
                    H * x1 : H * x1 + H, H * kind : H * kind + H
                ]
        exchange(
            lambda place, power=power: rows(send2[power], place),
            rows(recv2[power], me),
            rows(send2[power], me),
            rows(recv2[power], me),
            1 + power,
        )

    for power in range(3):
        pltpu.make_async_copy(recv2[power], recv2[power], got.at[1 + power]).wait()
        for x1 in range(2):
            kinds = [recv2[power][pl.ds(4 * x1 + kind, H, stride=8), :] for kind in range(4)]
            held = jnp.concatenate(
                [
                    jnp.concatenate([kinds[0], kinds[1]], axis=1),
                    jnp.concatenate([kinds[2], kinds[3]], axis=1),
                ],
                axis=0,
            )
            held = split(held)
            total = None
            for first, second, weight in PAIRS:
                if first != power:
                    continue
                part = product(held, table(4 + second), ROW_ROW)
                tidal = product(table(4 + 2 - first - second), split(part), ROW_COL)
                term = weight * (tidal * tidal)
                total = term if total is None else total + term
            if power == 0:
                shear_ref[x1] = total
            else:
                shear_ref[x1] = shear_ref[x1] + total

    for x1 in range(2):
        lines = product(split(shear_ref[x1]), table(7), COL_COL)
        both = product(table(8), split(lines), ROW_COL)
        for n in range(4):
            swapped = pltpu.roll(both[N:, H * n : H * n + H], 64, 1)
            lane = lax.broadcasted_iota(jnp.int32, (N, H), 1)
            send3[x1][:, H * n : H * n + H] = both[:N, H * n : H * n + H] + jnp.where(
                lane < 64, swapped, -swapped
            )

        def tile(place, x1=x1):
            return send3[x1].at[
                pl.ds(pl.multiple_of(place // 4 * 8, 8), 8),
                pl.ds(pl.multiple_of(place % 4 * H, H), H),
            ]

        exchange(tile, rows(recv3[x1], me), tile(me), rows(recv3[x1], me), 4 + x1)

    for x1 in range(2):
        pltpu.make_async_copy(recv3[x1], recv3[x1], got.at[4 + x1]).wait()
    line = lax.broadcasted_iota(jnp.int32, (H, H), 0)
    lane = lax.broadcasted_iota(jnp.int32, (H, H), 1)
    for b in range(8):
        plus = recv3[0][pl.ds(b, H, stride=8), :]
        minus = recv3[1][pl.ds(b, H, stride=8), :]
        even = jnp.where(line == 0, plus, plus + minus)
        odd = plus - minus
        swapped = pltpu.roll(odd, 64, 1)
        odd = jnp.where(line == 0, minus, jnp.where(lane < 64, swapped, -swapped))
        both = jnp.concatenate([even, odd], axis=0)
        done = product(split(both), table(9), COL_COL)
        real_part, imag_part = done[:64], done[64:]
        if b == 0:
            anchor = (
                (lax.broadcasted_iota(jnp.int32, (64, N), 0) == 0)
                & (lax.broadcasted_iota(jnp.int32, (64, N), 1) == 0)
                & (me == 0)
            )
            real_part = jnp.where(anchor, 0.0, real_part)
            imag_part = jnp.where(anchor, 0.0, imag_part)
        for part, value in enumerate((real_part, imag_part)):
            for side in range(2):
                final[2 * part + side][pl.ds(b, 64, stride=8), :] = value[
                    :, H * side : H * side + H
                ]
    stores = [
        pltpu.make_async_copy(
            final[2 * part + side],
            (real_out, imag_out)[part].at[:, pl.ds(H * side, H)],
            store_sem.at[2 * part + side],
        )
        for part in range(2)
        for side in range(2)
    ]
    for store in stores:
        store.start()

    for phase, ref in enumerate([send1] + list(send2) + list(recv3)):
        part = ref.at[pl.ds(0, 8 * (NUM - 1))]
        pltpu.make_async_copy(part, part, sent.at[phase]).wait()
    for store in stores:
        store.wait()


def per_device(density):
    arrays = [jnp.asarray(table) for table in tables()]
    buffer = pltpu.VMEM((8 * NUM, H), F32)
    result = jax.ShapeDtypeStruct((512, N), F32)
    real_part, imag_part = pl.pallas_call(
        body,
        out_shape=(result, result),
        in_specs=[pl.BlockSpec(memory_space=pltpu.VMEM)]
        + [pl.BlockSpec(memory_space=pl.ANY)] * 20,
        out_specs=[pl.BlockSpec(memory_space=pl.ANY)] * 2,
        scratch_shapes=[pltpu.VMEM(array.shape, BF16) for array in arrays]
        + [buffer, pltpu.VMEM((32, 32, H), F32)]
        + [buffer] * 6
        + [pltpu.VMEM((N, 512), F32)] * 2
        + [buffer] * 2
        + [pltpu.VMEM((512, H), F32)] * 4
        + [
            pltpu.VMEM((2, N, N), F32),
            pltpu.SemaphoreType.DMA((20,)),
            pltpu.SemaphoreType.DMA((4,)),
            pltpu.SemaphoreType.DMA((6,)),
            pltpu.SemaphoreType.DMA((6,)),
        ],
        compiler_params=pltpu.CompilerParams(
            collective_id=0, has_side_effects=True, vmem_limit_bytes=56 * 2**20
        ),
        name="tidal",
    )(density, *arrays)
    return real_part.reshape(64, 8, N), imag_part.reshape(64, 8, N)


def solution(mesh):
    return jax.shard_map(
        per_device,
        mesh=mesh,
        in_specs=(P("wide", "narrow", None),),
        out_specs=(P("narrow", "wide", None), P("narrow", "wide", None)),
        check_vma=False,
    )
```

time: 486 us -> 68.6 us (0.14)
  the two profiles are of different devices: /device:TPU:0 before, /device:TPU:1 now
where the time goes in v1:
time: 68.6 us; the launch traced here: 68.4 us
  Pallas kernels  65.1 us (95%)
  local copies, waits for them, and re-layouts  2.72 us (4%)
    pallas_call x1, Pallas kernels, per_device(): pl.pallas_call(body, out_shape=(result, result), in_specs=[pl.BlockSpec(m...  65.1 us
    unnamed x4, local copies, waits for them, and re-layouts  2.72 us

profile of v1, /device:TPU:1, one launch (start us, length us, event | category | flops | bytes accessed | tf_op | source)
XLA Modules:
  0.0 68.4 jit_solution(18040137833067807904)
XLA Ops:
  0.6 65.1 %tidal.1 = (f32[512,256]{1,0:T(8,128)}, f32[512,256]{1,0:T(8,128)}) custom-call(f32[8,64,256]{2,1,0:T(8,128)} %density.1, bf16[256,256]{1,0:T(8,128)(2,1)} %constant.40.clone.refs_0_, bf16[256,256]{1,0:T(8,128)(2,1)} %constant.41.clone.refs_1_, bf16[256,256]{1,0:T(8,128)(2,1)} %constant.42.clone.refs_2_, bf16[256,256]{1,0:T(8,128)(2,1)} %constant.43.clone.refs_3_, ...), custom_call_target="tpu_custom_call" | custom-call | tf_op jit(solution)/shard_map/tidal/pallas_call | solution.py:284
  65.7 0.0 copy-start
  65.7 1.9 %copy.25 = f32[64,8,256]{2,1,0:T(8,128)} copy(f32[64,8,256]{2,1,0:T(8,128)} %bitcast.3) | data formatting | bytes 1048576
  67.6 0.0 copy-done
  67.6 0.8 %copy.26 = f32[64,8,256]{2,1,0:T(8,128)} copy(f32[64,8,256]{2,1,0:T(8,128)S(1)} %bitcast.2) | data formatting | bytes 1048576
Async XLA Ops:
  65.7 1.9 %copy-start = (f32[512,256]{1,0:T(8,128)S(1)}, f32[512,256]{1,0:T(8,128)}, u32[]{:S(2)}) copy-start(f32[512,256]{1,0:T(8,128)} %get-tuple-element.5) | copy-start | bytes 1572868

commit v2 on v1

v2 whole, which is shorter than its diff:
```python
import math

import jax
import jax.numpy as jnp
import ml_dtypes
import numpy as np
from jax import lax
from jax.experimental import pallas as pl
from jax.experimental.pallas import tpu as pltpu
from jax.sharding import PartitionSpec as P

LOGICAL = pl.DeviceIdType.LOGICAL
BF16 = jnp.bfloat16
F32 = jnp.float32
N = 256
H = 128
STEP = 2.0 * math.pi / N
NUM = 128


def split_np(table):
    table = np.asarray(table, np.float32)
    high = table.astype(ml_dtypes.bfloat16)
    low = (table - high.astype(np.float32)).astype(ml_dtypes.bfloat16)
    return high, low


def angle(rows, cols):
    return (np.asarray(rows)[:, None] * np.asarray(cols)[None, :] % N) * STEP


def tables():
    half = np.arange(H)
    full = np.arange(N)
    slab = np.concatenate([half, [H], N - half[1:]])
    wave = half * STEP
    weight = np.where(half == 0, 1.0, 2.0) / N
    cos_sin = np.concatenate([np.cos(angle(half, full)), np.sin(angle(half, full))])

    def back(points, power):
        cosine = np.cos(angle(points, half)) * (weight * wave**power)
        sine = np.sin(angle(points, half)) * (weight * wave**power)
        if power == 1:
            return np.concatenate([sine, -cosine], axis=1)
        return np.concatenate([cosine, sine], axis=1)

    back_slab = [back(slab, power) for power in range(3)]
    back_full = [back(full, power) for power in range(3)]
    even = np.cos(angle(half, full))
    odd = np.sin(angle(half, full))
    odd[0] = np.where(full % 2 == 0, 1.0, -1.0)
    last_x = np.concatenate([even, odd]) / float(N) ** 1.5
    order = (
        np.arange(2)[:, None, None]
        + 2 * np.arange(4)[None, :, None]
        + 8 * np.arange(32)[None, None, :]
    ).reshape(-1)
    out = []
    for table in [cos_sin, cos_sin[:, order]] + back_slab + back_full + [last_x]:
        out += list(split_np(table))
    return out


def split(value):
    high = value.astype(BF16)
    low = (value - high.astype(F32)).astype(BF16)
    return high, low


def product(left, right, dims):
    def one(a, b):
        return lax.dot_general(a, b, (dims, ((), ())), preferred_element_type=F32)

    return one(left[0], right[0]) + (one(left[0], right[1]) + one(left[1], right[0]))


ROW_COL = ((1,), (0,))
ROW_ROW = ((1,), (1,))
PAIRS = ((0, 0, 1.0), (0, 1, 2.0), (0, 2, 1.0), (1, 0, 2.0), (1, 1, 2.0), (2, 0, 1.0))


def walk(me, visit):
    def step(_, place):
        place = place + 37
        place = jnp.where(place >= NUM, place - NUM, place)
        visit(place)
        return place

    lax.fori_loop(1, NUM, step, me, unroll=8)


TABLES = 18
PHASES = 9


def body(density, *refs):
    consts, refs = refs[:TABLES], refs[TABLES:]
    real_out, imag_out, refs = refs[0], refs[1], refs[2:]
    tabs, refs = refs[:TABLES], refs[TABLES:]
    send1, recv1 = refs[0], refs[1]
    send2, recv2 = refs[2:6], refs[6:10]
    send3, recv3 = refs[10:12], refs[12:14]
    final = refs[14:18]
    load_sem, store_sem, sent, got = refs[18:]
    wide = lax.axis_index("wide")
    narrow = lax.axis_index("narrow")
    me = wide * 4 + narrow

    barrier = pltpu.get_barrier_semaphore()

    def greet(place):
        pl.semaphore_signal(barrier, inc=1, device_id=place, device_id_type=LOGICAL)

    walk(me, greet)
    loads = [
        pltpu.make_async_copy(consts[i], tabs[i], load_sem.at[i]) for i in range(TABLES)
    ]
    for load in loads:
        load.start()

    def table(number, *index):
        return tabs[2 * number][index or ...], tabs[2 * number + 1][index or ...]

    def ready(number):
        loads[2 * number].wait()
        loads[2 * number + 1].wait()

    waits = []

    def exchange(source, target, whole, phase):
        pltpu.make_async_copy(source(me), target(me), got.at[phase]).start()

        def start(place):
            pltpu.make_async_remote_copy(
                src_ref=source(place),
                dst_ref=target(me),
                send_sem=sent.at[phase],
                recv_sem=got.at[phase],
                device_id=place,
                device_id_type=LOGICAL,
            ).start()

        walk(me, start)
        part = whole.at[pl.ds(0, NUM - 1)]
        waits.append(pltpu.make_async_copy(part, part, sent.at[phase]))

    def swap(send, recv, first, count, phase):
        exchange(
            lambda place: send.at[place, pl.ds(first, count)],
            lambda place: recv.at[place, pl.ds(first, count)],
            send.at[:, pl.ds(first, count)],
            phase,
        )

    def arrive(recv, first, count, phase):
        part = recv.at[:, pl.ds(first, count)]
        pltpu.make_async_copy(part, part, got.at[phase]).wait()

    def flat(ref):
        return ref.reshape(8 * NUM, H)

    ready(0)
    block = split(density[...].reshape(512, N))
    for part in range(2):
        lines = product(table(0, pl.ds(H * part, H)), block, ROW_ROW)
        for q in range(4):
            flat(send1)[pl.ds(4 * part + q, H, stride=8), :] = lines[:, H * q : H * q + H]
        if part == 0:
            pl.semaphore_wait(barrier, NUM - 1)
        swap(send1, recv1, 4 * part, 4, part)

    for number in range(1, TABLES // 2):
        ready(number)
    wave_a = lax.broadcasted_iota(jnp.int32, (H, H), 0).astype(F32) * STEP
    wave_b = lax.broadcasted_iota(jnp.int32, (H, H), 1).astype(F32) * STEP
    wave_c = me.astype(F32) * STEP
    squared = wave_a * wave_a + wave_b * wave_b + wave_c * wave_c
    smooth = jnp.where(
        squared > 0, jnp.exp(-0.5 * squared) / jnp.where(squared > 0, squared, 1.0), 0.0
    )
    smooth = jnp.concatenate([smooth, smooth], axis=0)
    smooth = jnp.concatenate([smooth, smooth], axis=1)

    def back_x(filtered, part, x1):
        for power in range(3):
            field = product(table(2 + power, pl.ds(H * x1, H)), filtered, ROW_COL)
            for s in range(2):
                if x1 == 0:
                    ref, row = send2[part], 2 * power + s
                else:
                    ref, row = send2[2 + power // 2], 4 * (power % 2) + 2 * part + s
                flat(ref)[pl.ds(row, H, stride=8), :] = field[:, H * s : H * s + H]

    kept = []
    for part in range(2):
        arrive(recv1, 4 * part, 4, part)
        pieces = []
        for n in range(4):
            pieces.append(
                jnp.concatenate(
                    [
                        flat(recv1)[pl.ds(8 * n + 4 * part + q, 32, stride=32), :]
                        for q in range(4)
                    ],
                    axis=0,
                )
            )
        plane = jnp.concatenate(
            [
                jnp.concatenate([piece[:, 64 * low : 64 * low + 64] for piece in pieces], axis=1)
                for low in range(2)
            ],
            axis=0,
        )
        along_x = product(table(1), split(plane), ROW_COL)
        along_y = product(split(along_x), table(0), ROW_ROW)
        filtered = split(along_y * smooth)
        kept.append(filtered)
        back_x(filtered, part, 0)
        swap(send2[part], recv2[part], 0, 6, 2 + part)
    for part in range(2):
        back_x(kept[part], part, 1)
    for power in range(3):
        swap(send2[2 + power // 2], recv2[2 + power // 2], 4 * (power % 2), 4, 4 + power)

    flip_lane = 1.0 - 2.0 * (lax.broadcasted_iota(jnp.int32, (1, N), 1) & 1).astype(F32)
    flip_line = 1.0 - 2.0 * (lax.broadcasted_iota(jnp.int32, (N, 1), 0) & 1).astype(F32)

    for x1 in range(2):
        if x1 == 0:
            arrive(recv2[0], 0, 6, 2)
            arrive(recv2[1], 0, 6, 3)
        shear = None
        for power in range(3):
            if x1 == 1:
                arrive(recv2[2 + power // 2], 4 * (power % 2), 4, 4 + power)
            halves = []
            for part in range(2):
                if x1 == 0:
                    ref, row = recv2[part], 2 * power
                else:
                    ref, row = recv2[2 + power // 2], 4 * (power % 2) + 2 * part
                halves.append(
                    jnp.concatenate(
                        [flat(ref)[pl.ds(row + s, H, stride=8), :] for s in range(2)], axis=1
                    )
                )
            held = split(jnp.concatenate(halves, axis=0))
            for first, second, weight in PAIRS:
                if first != power:
                    continue
                back_y = product(held, table(5 + second), ROW_ROW)
                tidal = product(table(5 + 2 - first - second), split(back_y), ROW_COL)
                term = weight * (tidal * tidal)
                shear = term if shear is None else shear + term
        turned = jnp.transpose(shear)
        lines = []
        for high in range(2):
            lines.append(product(split(turned), table(0), ROW_ROW))
            turned = turned * flip_lane
        lines = jnp.concatenate(lines, axis=1)
        for high in range(2):
            both = product(table(0), split(lines), ROW_COL)
            lines = lines * flip_line
            for side in range(2):
                cosine = both[:H, N * side : N * side + N]
                sine = both[H:, N * side : N * side + N]
                real_part = cosine[:, :H] - sine[:, H:]
                imag_part = -(cosine[:, H:] + sine[:, :H])
                for n in range(2):
                    here = slice(64 * n, 64 * n + 64)
                    send3[x1][H * high : H * high + H, pl.ds(N * side + H * n, H)] = (
                        jnp.concatenate([real_part[:, here], imag_part[:, here]], axis=1)
                    )

        def tile(place, x1=x1):
            return send3[x1].at[
                pl.ds(pl.multiple_of(place // 4 * 8, 8), 8),
                pl.ds(pl.multiple_of(place % 4 * H, H), H),
            ]

        exchange(tile, lambda place, x1=x1: recv3[x1].at[place], recv3[x1], 7 + x1)

    arrive(recv3[0], 0, 8, 7)
    arrive(recv3[1], 0, 8, 8)
    line = lax.broadcasted_iota(jnp.int32, (H, H), 0)
    lane = lax.broadcasted_iota(jnp.int32, (H, H), 1)
    for b in range(8):
        plus = flat(recv3[0])[pl.ds(b, H, stride=8), :]
        minus = flat(recv3[1])[pl.ds(b, H, stride=8), :]
        even = jnp.where(line == 0, plus, plus + minus)
        odd = plus - minus
        swapped = pltpu.roll(odd, 64, 1)
        odd = jnp.where(line == 0, minus, jnp.where(lane < 64, swapped, -swapped))
        both = jnp.concatenate([even, odd], axis=0)
        done = product(split(jnp.transpose(both)), table(8), ROW_COL)
        real_part, imag_part = done[:64], done[64:]
        if b == 0:
            anchor = (
                (lax.broadcasted_iota(jnp.int32, (64, N), 0) == 0)
                & (lax.broadcasted_iota(jnp.int32, (64, N), 1) == 0)
                & (me == 0)
            )
            real_part = jnp.where(anchor, 0.0, real_part)
            imag_part = jnp.where(anchor, 0.0, imag_part)
        for part, value in enumerate((real_part, imag_part)):
            for side in range(2):
                final[2 * part + side][pl.ds(b, 64, stride=8), :] = value[
                    :, H * side : H * side + H
                ]
    stores = [
        pltpu.make_async_copy(
            final[2 * part + side],
            (real_out, imag_out)[part].at[:, pl.ds(H * side, H)],
            store_sem.at[2 * part + side],
        )
        for part in range(2)
        for side in range(2)
    ]
    for store in stores:
        store.start()
    for wait in waits:
        wait.wait()
    for store in stores:
        store.wait()


def per_device(density):
    arrays = [jnp.asarray(table) for table in tables()]
    buffer = pltpu.VMEM((NUM, 8, H), F32)
    result = jax.ShapeDtypeStruct((512, N), F32)
    real_part, imag_part = pl.pallas_call(
        body,
        out_shape=(result, result),
        in_specs=[pl.BlockSpec(memory_space=pltpu.VMEM)]
        + [pl.BlockSpec(memory_space=pl.ANY)] * TABLES,
        out_specs=[pl.BlockSpec(memory_space=pl.ANY)] * 2,
        scratch_shapes=[pltpu.VMEM(array.shape, BF16) for array in arrays]
        + [buffer] * 10
        + [pltpu.VMEM((N, 512), F32)] * 2
        + [buffer] * 2
        + [pltpu.VMEM((512, H), F32)] * 4
        + [
            pltpu.SemaphoreType.DMA((TABLES,)),
            pltpu.SemaphoreType.DMA((4,)),
            pltpu.SemaphoreType.DMA((PHASES,)),
            pltpu.SemaphoreType.DMA((PHASES,)),
        ],
        compiler_params=pltpu.CompilerParams(
            collective_id=0, has_side_effects=True, vmem_limit_bytes=56 * 2**20
        ),
        name="tidal",
    )(density, *arrays)
    return real_part.reshape(64, 8, N), imag_part.reshape(64, 8, N)


def solution(mesh):
    return jax.shard_map(
        per_device,
        mesh=mesh,
        in_specs=(P("wide", "narrow", None),),
        out_specs=(P("narrow", "wide", None), P("narrow", "wide", None)),
        check_vma=False,
    )
```

time: 68.6 us -> 59.6 us (0.87)
  Pallas kernels: 65.1 us -> 56 us
    pallas_call x1, Pallas kernels: 65.1 us -> 56 us  [per_device(): pl.pallas_call(body, out_shape=(result, result), in_specs=[pl.BlockSpec(m...]
where the time goes in v2:
time: 59.6 us; the launch traced here: 59.4 us
  Pallas kernels  56 us (94%)
  local copies, waits for them, and re-layouts  2.72 us (5%)
  between operations  0.65 us (1%)
    pallas_call x1, Pallas kernels, per_device(): pl.pallas_call(body, out_shape=(result, result), in_specs=[pl.BlockSpec(m...  56 us
    unnamed x4, local copies, waits for them, and re-layouts  2.72 us

profile of v2, /device:TPU:1, one launch (start us, length us, event | category | flops | bytes accessed | tf_op | source)
XLA Modules:
  0.0 59.4 jit_solution(16840044212665261592)
XLA Ops:
  0.6 56.0 %tidal.1 = (f32[512,256]{1,0:T(8,128)}, f32[512,256]{1,0:T(8,128)}) custom-call(f32[8,64,256]{2,1,0:T(8,128)} %density.1, bf16[256,256]{1,0:T(8,128)(2,1)} %constant.36.clone.refs_0_, bf16[256,256]{1,0:T(8,128)(2,1)} %constant.37.clone.refs_1_, bf16[256,256]{1,0:T(8,128)(2,1)} %constant.38.clone.refs_2_, bf16[256,256]{1,0:T(8,128)(2,1)} %constant.39.clone.refs_3_, ...), custom_call_target="tpu_custom_call" | custom-call | tf_op jit(solution)/shard_map/tidal/pallas_call | solution.py:332
  56.6 0.0 copy-start
  56.6 1.9 %copy.23 = f32[64,8,256]{2,1,0:T(8,128)} copy(f32[64,8,256]{2,1,0:T(8,128)} %bitcast.3) | data formatting | bytes 1048576
  58.6 0.0 copy-done
  58.6 0.8 %copy.24 = f32[64,8,256]{2,1,0:T(8,128)} copy(f32[64,8,256]{2,1,0:T(8,128)S(1)} %bitcast.2) | data formatting | bytes 1048576
Async XLA Ops:
  56.6 1.9 %copy-start = (f32[512,256]{1,0:T(8,128)S(1)}, f32[512,256]{1,0:T(8,128)}, u32[]{:S(2)}) copy-start(f32[512,256]{1,0:T(8,128)} %get-tuple-element.5) | copy-start | bytes 1572868

commit v3 on v2

--- a/solution.py
+++ b/solution.py
@@ -89,23 +89,25 @@
     lax.fori_loop(1, NUM, step, me, unroll=8)
 
 
-TABLES = 18
+TABLES = 16
+OUT = jax.ShapeDtypeStruct((NUM, 8, H), F32)
 PHASES = 9
 
 
 def body(density, *refs):
-    consts, refs = refs[:TABLES], refs[TABLES:]
-    real_out, imag_out, refs = refs[0], refs[1], refs[2:]
+    consts, refs = refs[0], refs[1:]
+    recv3, refs = refs[:2], refs[2:]
     tabs, refs = refs[:TABLES], refs[TABLES:]
     send1, recv1 = refs[0], refs[1]
     send2, recv2 = refs[2:6], refs[6:10]
-    send3, recv3 = refs[10:12], refs[12:14]
-    final = refs[14:18]
-    load_sem, store_sem, sent, got = refs[18:]
+    send3 = refs[10:12]
+    field, field_sem, load_sem, sent, got = refs[12:]
     wide = lax.axis_index("wide")
     narrow = lax.axis_index("narrow")
     me = wide * 4 + narrow
 
+    fetch = pltpu.make_async_copy(density, field, field_sem)
+    fetch.start()
     barrier = pltpu.get_barrier_semaphore()
 
     def greet(place):
@@ -113,7 +115,8 @@
 
     walk(me, greet)
     loads = [
-        pltpu.make_async_copy(consts[i], tabs[i], load_sem.at[i]) for i in range(TABLES)
+        pltpu.make_async_copy(consts.at[pl.ds(N * i, N)], tabs[i], load_sem.at[i])
+        for i in range(TABLES)
     ]
     for load in loads:
         load.start()
@@ -160,7 +163,8 @@
         return ref.reshape(8 * NUM, H)
 
     ready(0)
-    block = split(density[...].reshape(512, N))
+    fetch.wait()
+    block = split(field[...].reshape(512, N))
     for part in range(2):
         lines = product(table(0, pl.ds(H * part, H)), block, ROW_ROW)
         for q in range(4):
@@ -283,6 +287,17 @@
 
     arrive(recv3[0], 0, 8, 7)
     arrive(recv3[1], 0, 8, 8)
+    for wait in waits:
+        wait.wait()
+
+def finish(first, second, high, low, real_out, imag_out, *refs):
+    final, store_sem = refs[:4], refs[4]
+    me = lax.axis_index("wide") * 4 + lax.axis_index("narrow")
+    recv3 = (first, second)
+
+    def flat(ref):
+        return ref.reshape(8 * NUM, H)
+
     line = lax.broadcasted_iota(jnp.int32, (H, H), 0)
     lane = lax.broadcasted_iota(jnp.int32, (H, H), 1)
     for b in range(8):
@@ -293,7 +308,7 @@
         swapped = pltpu.roll(odd, 64, 1)
         odd = jnp.where(line == 0, minus, jnp.where(lane < 64, swapped, -swapped))
         both = jnp.concatenate([even, odd], axis=0)
-        done = product(split(jnp.transpose(both)), table(8), ROW_COL)
+        done = product(split(jnp.transpose(both)), (high[...], low[...]), ROW_COL)
         real_part, imag_part = done[:64], done[64:]
         if b == 0:
             anchor = (
@@ -319,38 +334,45 @@
     ]
     for store in stores:
         store.start()
-    for wait in waits:
-        wait.wait()
     for store in stores:
         store.wait()
 
 
 def per_device(density):
     arrays = [jnp.asarray(table) for table in tables()]
+    last = arrays[TABLES:]
+    joined = jnp.asarray(np.concatenate(tables()[:TABLES]))
     buffer = pltpu.VMEM((NUM, 8, H), F32)
-    result = jax.ShapeDtypeStruct((512, N), F32)
-    real_part, imag_part = pl.pallas_call(
+    held = pl.pallas_call(
         body,
-        out_shape=(result, result),
-        in_specs=[pl.BlockSpec(memory_space=pltpu.VMEM)]
-        + [pl.BlockSpec(memory_space=pl.ANY)] * TABLES,
-        out_specs=[pl.BlockSpec(memory_space=pl.ANY)] * 2,
-        scratch_shapes=[pltpu.VMEM(array.shape, BF16) for array in arrays]
+        out_shape=(OUT, OUT),
+        in_specs=[pl.BlockSpec(memory_space=pl.ANY)] * 2,
+        out_specs=[pl.BlockSpec(memory_space=pltpu.VMEM)] * 2,
+        scratch_shapes=[pltpu.VMEM((N, N), BF16)] * TABLES
         + [buffer] * 10
         + [pltpu.VMEM((N, 512), F32)] * 2
-        + [buffer] * 2
-        + [pltpu.VMEM((512, H), F32)] * 4
         + [
+            pltpu.VMEM(density.shape, F32),
+            pltpu.SemaphoreType.DMA,
             pltpu.SemaphoreType.DMA((TABLES,)),
-            pltpu.SemaphoreType.DMA((4,)),
             pltpu.SemaphoreType.DMA((PHASES,)),
             pltpu.SemaphoreType.DMA((PHASES,)),
         ],
         compiler_params=pltpu.CompilerParams(
-            collective_id=0, has_side_effects=True, vmem_limit_bytes=56 * 2**20
+            collective_id=0, has_side_effects=True, vmem_limit_bytes=55259955
         ),
         name="tidal",
-    )(density, *arrays)
+    )(density, joined)
+    result = jax.ShapeDtypeStruct((512, N), F32)
+    real_part, imag_part = pl.pallas_call(
+        finish,
+        out_shape=(result, result),
+        in_specs=[pl.BlockSpec(memory_space=pltpu.VMEM)] * 4,
+        out_specs=[pl.BlockSpec(memory_space=pl.ANY)] * 2,
+        scratch_shapes=[pltpu.VMEM((512, H), F32)] * 4 + [pltpu.SemaphoreType.DMA((4,))],
+        compiler_params=pltpu.CompilerParams(vmem_limit_bytes=16 * 2**20),
+        name="finish",
+    )(*held, *last)
     return real_part.reshape(64, 8, N), imag_part.reshape(64, 8, N)
 
 

time: 59.6 us -> 55.9 us (0.938)
  local copies, waits for them, and re-layouts: 2.72 us -> 0.01 us
  Pallas kernels: 56 us -> 55 us
    unnamed x4, local copies, waits for them, and re-layouts: 2.72 us -> 0.01 us
    pallas_call x1 -> x2, Pallas kernels: 56 us -> 55 us  [the longest x1 53.1 us: per_device(): pl.pallas_call(body, out_shape=(OUT, OUT), in_specs=[pl.BlockSpec(memory_...]
where the time goes in v3:
time: 55.9 us; the launch traced here: 55.7 us
  Pallas kernels  55 us (98%)
  between operations  0.67 us (1%)
    pallas_call x1, Pallas kernels, per_device(): pl.pallas_call(body, out_shape=(OUT, OUT), in_specs=[pl.BlockSpec(memory_...  53.1 us
    pallas_call x1, Pallas kernels, per_device(): pl.pallas_call(finish, out_shape=(result, result), in_specs=[pl.BlockSpec...  1.95 us

profile of v3, /device:TPU:1, one launch (start us, length us, event | category | flops | bytes accessed | tf_op | source)
XLA Modules:
  0.0 55.7 jit_solution(18022679388508365975)
XLA Ops:
  0.6 0.0 copy-start
  0.6 0.0 copy-start.1
  0.7 53.1 %tidal.1 = (f32[128,8,128]{2,1,0:T(8,128)S(1)}, f32[128,8,128]{2,1,0:T(8,128)S(1)}) custom-call(f32[8,64,256]{2,1,0:T(8,128)} %density.1, bf16[4096,256]{1,0:T(8,128)(2,1)} %constant.8.clone.refs_0_), custom_call_target="tpu_custom_call" | custom-call | tf_op jit(solution)/shard_map/tidal/pallas_call | solution.py:346
  53.8 0.0 copy-done
  53.8 0.0 copy-done.1
  53.8 2.0 %finish.1 = (f32[512,256]{1,0:T(8,128)}, f32[512,256]{1,0:T(8,128)}) custom-call(f32[128,8,128]{2,1,0:T(8,128)S(1)} %get-tuple-element.6.first, f32[128,8,128]{2,1,0:T(8,128)S(1)} %get-tuple-element.7.second, bf16[256,256]{1,0:T(8,128)(2,1)S(1)} %copy-done.1, bf16[256,256]{1,0:T(8,128)(2,1)S(1)} %copy-done), custom_call_target="tpu_custom_call" | custom-call | tf_op jit(solution)/shard_map/finish/pallas_call | solution.py:367
Async XLA Ops:
  0.6 53.1 %copy-start = (bf16[256,256]{1,0:T(8,128)(2,1)S(1)}, bf16[256,256]{1,0:T(8,128)(2,1)}, u32[]{:S(2)}) copy-start(bf16[256,256]{1,0:T(8,128)(2,1)} %constant.7.clone.low) | copy-start | bytes 393220
  0.6 53.1 %copy-start.1 = (bf16[256,256]{1,0:T(8,128)(2,1)S(1)}, bf16[256,256]{1,0:T(8,128)(2,1)}, u32[]{:S(2)}) copy-start(bf16[256,256]{1,0:T(8,128)(2,1)} %constant.6.clone.high) | copy-start | bytes 393220

commit v4 on v3

--- a/solution.py
+++ b/solution.py
@@ -1,4 +1,5 @@
 import math
+import random
 
 import jax
 import jax.numpy as jnp
@@ -79,6 +80,40 @@
 PAIRS = ((0, 0, 1.0), (0, 1, 2.0), (0, 2, 1.0), (1, 0, 2.0), (1, 1, 2.0), (2, 0, 1.0))
 
 
+def hops(offset):
+    return sum(min(step, 4 - step) for step in offset[:3])
+
+
+def order():
+    offsets = [
+        (x, y, z, core)
+        for x in range(4)
+        for y in range(4)
+        for z in range(4)
+        for core in range(2)
+        if x + y + z + core > 0
+    ]
+    random.Random(1).shuffle(offsets)
+    return sorted(offsets, key=lambda offset: hops(offset) < 4)
+
+
+ORDER = order()
+
+
+def places(wide, narrow):
+    x, y = lax.rem(wide, 4), lax.rem(lax.div(wide, 4), 4)
+    z = 2 * lax.div(wide, 16) + lax.div(narrow, 2)
+    core = lax.rem(narrow, 2)
+    along_x = [4 * lax.rem(x + step, 4) for step in range(4)]
+    along_y = [16 * lax.rem(y + step, 4) for step in range(4)]
+    along_z = []
+    for step in range(4):
+        there = lax.rem(z + step, 4)
+        along_z.append(64 * lax.div(there, 2) + 2 * lax.rem(there, 2))
+    cores = [core, 1 - core]
+    return [along_x[a] + along_y[b] + along_z[c] + cores[d] for a, b, c, d in ORDER]
+
+
 def walk(me, visit):
     def step(_, place):
         place = place + 37
@@ -92,6 +127,7 @@
 TABLES = 16
 OUT = jax.ShapeDtypeStruct((NUM, 8, H), F32)
 PHASES = 9
+DISTANT_FIRST = (0, 1, 5, 6, 8)
 
 
 def body(density, *refs):
@@ -113,6 +149,7 @@
     def greet(place):
         pl.semaphore_signal(barrier, inc=1, device_id=place, device_id_type=LOGICAL)
 
+    others = places(wide, narrow)
     walk(me, greet)
     loads = [
         pltpu.make_async_copy(consts.at[pl.ds(N * i, N)], tabs[i], load_sem.at[i])
@@ -143,7 +180,11 @@
                 device_id_type=LOGICAL,
             ).start()
 
-        walk(me, start)
+        if phase in DISTANT_FIRST:
+            for place in others:
+                start(place)
+        else:
+            walk(me, start)
         part = whole.at[pl.ds(0, NUM - 1)]
         waits.append(pltpu.make_async_copy(part, part, sent.at[phase]))
 

time: 55.9 us -> 55 us (0.984)
  Pallas kernels: 55 us -> 54.2 us
    pallas_call x1, Pallas kernels: 53.1 us -> 52.3 us  [per_device(): pl.pallas_call(body, out_shape=(OUT, OUT), in_specs=[pl.BlockSpec(memory_...]
where the time goes in v4:
time: 55 us; the launch traced here: 54.9 us
  Pallas kernels  54.2 us (99%)
  between operations  0.67 us (1%)
    pallas_call x1, Pallas kernels, per_device(): pl.pallas_call(body, out_shape=(OUT, OUT), in_specs=[pl.BlockSpec(memory_...  52.3 us
    pallas_call x1, Pallas kernels, per_device(): pl.pallas_call(finish, out_shape=(result, result), in_specs=[pl.BlockSpec...  1.95 us

profile of v4, /device:TPU:1, one launch (start us, length us, event | category | flops | bytes accessed | tf_op | source)
XLA Modules:
  0.0 54.9 jit_solution(4952417590435431891)
XLA Ops:
  0.6 0.0 copy-start
  0.6 0.0 copy-start.1
  0.7 52.3 %tidal.1 = (f32[128,8,128]{2,1,0:T(8,128)S(1)}, f32[128,8,128]{2,1,0:T(8,128)S(1)}) custom-call(f32[8,64,256]{2,1,0:T(8,128)} %density.1, bf16[4096,256]{1,0:T(8,128)(2,1)} %constant.8.clone.refs_0_), custom_call_target="tpu_custom_call" | custom-call | tf_op jit(solution)/shard_map/tidal/pallas_call | solution.py:387
  52.9 0.0 copy-done
  52.9 0.0 copy-done.1
  53.0 1.9 %finish.1 = (f32[512,256]{1,0:T(8,128)}, f32[512,256]{1,0:T(8,128)}) custom-call(f32[128,8,128]{2,1,0:T(8,128)S(1)} %get-tuple-element.6.first, f32[128,8,128]{2,1,0:T(8,128)S(1)} %get-tuple-element.7.second, bf16[256,256]{1,0:T(8,128)(2,1)S(1)} %copy-done.1, bf16[256,256]{1,0:T(8,128)(2,1)S(1)} %copy-done), custom_call_target="tpu_custom_call" | custom-call | tf_op jit(solution)/shard_map/finish/pallas_call | solution.py:408
Async XLA Ops:
  0.6 52.3 %copy-start = (bf16[256,256]{1,0:T(8,128)(2,1)S(1)}, bf16[256,256]{1,0:T(8,128)(2,1)}, u32[]{:S(2)}) copy-start(bf16[256,256]{1,0:T(8,128)(2,1)} %constant.7.clone.low) | copy-start | bytes 393220
  0.6 52.3 %copy-start.1 = (bf16[256,256]{1,0:T(8,128)(2,1)S(1)}, bf16[256,256]{1,0:T(8,128)(2,1)}, u32[]{:S(2)}) copy-start(bf16[256,256]{1,0:T(8,128)(2,1)} %constant.6.clone.high) | copy-start | bytes 393220

commit v5 on v4

--- a/solution.py
+++ b/solution.py
@@ -94,7 +94,7 @@
         if x + y + z + core > 0
     ]
     random.Random(1).shuffle(offsets)
-    return sorted(offsets, key=lambda offset: hops(offset) < 4)
+    return sorted(offsets, key=lambda offset: -hops(offset))
 
 
 ORDER = order()
@@ -127,7 +127,7 @@
 TABLES = 16
 OUT = jax.ShapeDtypeStruct((NUM, 8, H), F32)
 PHASES = 9
-DISTANT_FIRST = (0, 1, 5, 6, 8)
+DISTANT_FIRST = (0, 6, 8)
 
 
 def body(density, *refs):
@@ -144,18 +144,21 @@
 
     fetch = pltpu.make_async_copy(density, field, field_sem)
     fetch.start()
-    barrier = pltpu.get_barrier_semaphore()
-
-    def greet(place):
-        pl.semaphore_signal(barrier, inc=1, device_id=place, device_id_type=LOGICAL)
-
-    others = places(wide, narrow)
-    walk(me, greet)
     loads = [
         pltpu.make_async_copy(consts.at[pl.ds(N * i, N)], tabs[i], load_sem.at[i])
         for i in range(TABLES)
     ]
-    for load in loads:
+    for load in loads[:2]:
+        load.start()
+    barrier = pltpu.get_barrier_semaphore()
+
+    def greet(place):
+        pl.semaphore_signal(barrier, inc=1, device_id=place, device_id_type=LOGICAL)
+
+    others = places(wide, narrow)
+    for place in others:
+        greet(place)
+    for load in loads[2:]:
         load.start()
 
     def table(number, *index):
@@ -341,6 +344,7 @@
 
     line = lax.broadcasted_iota(jnp.int32, (H, H), 0)
     lane = lax.broadcasted_iota(jnp.int32, (H, H), 1)
+    turned = []
     for b in range(8):
         plus = flat(recv3[0])[pl.ds(b, H, stride=8), :]
         minus = flat(recv3[1])[pl.ds(b, H, stride=8), :]
@@ -348,33 +352,34 @@
         odd = plus - minus
         swapped = pltpu.roll(odd, 64, 1)
         odd = jnp.where(line == 0, minus, jnp.where(lane < 64, swapped, -swapped))
-        both = jnp.concatenate([even, odd], axis=0)
-        done = product(split(jnp.transpose(both)), (high[...], low[...]), ROW_COL)
-        real_part, imag_part = done[:64], done[64:]
-        if b == 0:
-            anchor = (
-                (lax.broadcasted_iota(jnp.int32, (64, N), 0) == 0)
-                & (lax.broadcasted_iota(jnp.int32, (64, N), 1) == 0)
-                & (me == 0)
-            )
-            real_part = jnp.where(anchor, 0.0, real_part)
-            imag_part = jnp.where(anchor, 0.0, imag_part)
-        for part, value in enumerate((real_part, imag_part)):
+        turned.append(jnp.transpose(jnp.concatenate([even, odd], axis=0)))
+    anchor = (
+        (lax.broadcasted_iota(jnp.int32, (32, N), 0) == 0)
+        & (lax.broadcasted_iota(jnp.int32, (32, N), 1) == 0)
+        & (me == 0)
+    )
+    stores = []
+    for piece in range(2):
+        for part in range(2):
+            first = 64 * part + 32 * piece
+            rows = jnp.concatenate([block[first : first + 32] for block in turned], axis=0)
+            done = product(split(rows), (high[...], low[...]), ROW_COL)
+            for b in range(8):
+                value = done[32 * b : 32 * b + 32]
+                if b == 0 and piece == 0:
+                    value = jnp.where(anchor, 0.0, value)
+                for side in range(2):
+                    final[2 * part + side][pl.ds(N * piece + b, 32, stride=8), :] = value[
+                        :, H * side : H * side + H
+                    ]
             for side in range(2):
-                final[2 * part + side][pl.ds(b, 64, stride=8), :] = value[
-                    :, H * side : H * side + H
-                ]
-    stores = [
-        pltpu.make_async_copy(
-            final[2 * part + side],
-            (real_out, imag_out)[part].at[:, pl.ds(H * side, H)],
-            store_sem.at[2 * part + side],
-        )
-        for part in range(2)
-        for side in range(2)
-    ]
-    for store in stores:
-        store.start()
+                store = pltpu.make_async_copy(
+                    final[2 * part + side].at[pl.ds(N * piece, N)],
+                    (real_out, imag_out)[part].at[pl.ds(N * piece, N), pl.ds(H * side, H)],
+                    store_sem.at[len(stores)],
+                )
+                store.start()
+                stores.append(store)
     for store in stores:
         store.wait()
 
@@ -410,7 +415,7 @@
         out_shape=(result, result),
         in_specs=[pl.BlockSpec(memory_space=pltpu.VMEM)] * 4,
         out_specs=[pl.BlockSpec(memory_space=pl.ANY)] * 2,
-        scratch_shapes=[pltpu.VMEM((512, H), F32)] * 4 + [pltpu.SemaphoreType.DMA((4,))],
+        scratch_shapes=[pltpu.VMEM((512, H), F32)] * 4 + [pltpu.SemaphoreType.DMA((8,))],
         compiler_params=pltpu.CompilerParams(vmem_limit_bytes=16 * 2**20),
         name="finish",
     )(*held, *last)

time: 55 us -> 53.5 us (0.973)
  Pallas kernels: 54.2 us -> 52.7 us
    pallas_call x1, Pallas kernels: 52.3 us -> 50.8 us  [per_device(): pl.pallas_call(body, out_shape=(OUT, OUT), in_specs=[pl.BlockSpec(memory_...]
where the time goes in v5:
time: 53.5 us; the launch traced here: 53.4 us
  Pallas kernels  52.7 us (99%)
  between operations  0.67 us (1%)
    pallas_call x1, Pallas kernels, per_device(): pl.pallas_call(body, out_shape=(OUT, OUT), in_specs=[pl.BlockSpec(memory_...  50.8 us
    pallas_call x1, Pallas kernels, per_device(): pl.pallas_call(finish, out_shape=(result, result), in_specs=[pl.BlockSpec...  1.89 us

profile of v5, /device:TPU:1, one launch (start us, length us, event | category | flops | bytes accessed | tf_op | source)
XLA Modules:
  0.0 53.4 jit_solution(17052659604360756638)
XLA Ops:
  0.6 0.0 copy-start
  0.6 0.0 copy-start.1
  0.7 50.8 %tidal.1 = (f32[128,8,128]{2,1,0:T(8,128)S(1)}, f32[128,8,128]{2,1,0:T(8,128)S(1)}) custom-call(f32[8,64,256]{2,1,0:T(8,128)} %density.1, bf16[4096,256]{1,0:T(8,128)(2,1)} %constant.8.clone.refs_0_), custom_call_target="tpu_custom_call" | custom-call | tf_op jit(solution)/shard_map/tidal/pallas_call | solution.py:392
  51.5 0.0 copy-done
  51.5 0.0 copy-done.1
  51.5 1.9 %finish.1 = (f32[512,256]{1,0:T(8,128)}, f32[512,256]{1,0:T(8,128)}) custom-call(f32[128,8,128]{2,1,0:T(8,128)S(1)} %get-tuple-element.6.first, f32[128,8,128]{2,1,0:T(8,128)S(1)} %get-tuple-element.7.second, bf16[256,256]{1,0:T(8,128)(2,1)S(1)} %copy-done.1, bf16[256,256]{1,0:T(8,128)(2,1)S(1)} %copy-done), custom_call_target="tpu_custom_call" | custom-call | tf_op jit(solution)/shard_map/finish/pallas_call | solution.py:413
Async XLA Ops:
  0.6 50.8 %copy-start = (bf16[256,256]{1,0:T(8,128)(2,1)S(1)}, bf16[256,256]{1,0:T(8,128)(2,1)}, u32[]{:S(2)}) copy-start(bf16[256,256]{1,0:T(8,128)(2,1)} %constant.7.clone.low) | copy-start | bytes 393220
  0.6 50.8 %copy-start.1 = (bf16[256,256]{1,0:T(8,128)(2,1)S(1)}, bf16[256,256]{1,0:T(8,128)(2,1)}, u32[]{:S(2)}) copy-start(bf16[256,256]{1,0:T(8,128)(2,1)} %constant.6.clone.high) | copy-start | bytes 393220
